TPU v7x, 32 devices: a whole 2x2x4 slice. The times are simulated.
32 devices in a mesh: row: 4 (over z), col: 2 (over x), pole: 4 (over y, core).
Axes of the slice: x: 2, y: 2, z: 4, core: 2. Of those that a mesh axis runs over, the one named last changes fastest.
Arguments:
- window: bfloat16 [4, 8192, 8192], P('pole', 'col', 'row'), may hold values from -6 to 6
- panels: bfloat16 [4, 2, 8192, 256], P('pole', 'col', 'row'), may hold values from -0.0625 to 0.0625
- row_map: int32 [3, 8192], P(None, 'row'), may hold values from 0 to 8191, as said below
- panel_root: int32 [4, 3], P('pole'), may hold values from 0 to 1
- upper_blocks: bfloat16 [4, 3, 256, 256], P('pole', None, 'row'), may hold values from -0.375 to 0.375
- diag_inverse: float32 [4, 3, 256, 256], P('pole', None, 'row'), may hold values from -6 to 6
- weights: float32 [4], replicated, may hold values from 0.25 to 1
- pole_order: int32 [4], P('pole'), may hold values from 0 to 3, each once
Outputs:
- inv_columns: float32 [3, 2, 4096, 256], P(None, 'col', ('row', 'pole'))
- inv_diag: float32 [3, 256, 256], P(None, ('row', 'pole'))
Inputs may be any that keep to these rules, and one draw needn't show every extreme that they name: row_map[k] permutes the positions inside each aligned group of 1024 consecutive positions. `pole_order`: each of the 4 poles appears once.
All inputs are finite; a program needn't handle non-finite values.
Results may differ from a plain program's by a relative error of at most 0.0003.
Values may be sent and summed in bfloat16 or wider, within the bound.
A program may use at most 128 MiB of HBM per device.

v0:
```python
import jax
import jax.numpy as jnp
from jax import lax
from jax.sharding import PartitionSpec as P

NS = 3


def precise(left, right):
    return jnp.dot(left, right, precision=lax.Precision.HIGHEST, preferred_element_type=jnp.float32)


def pair_index(current, earlier):
    return current * (current - 1) // 2 + earlier


def inverse_block(diagonals, crossed, first, second):
    if first == second:
        return diagonals[first]
    if first < second:
        return crossed[first, second]
    return crossed[second, first].T


def window_term(window_block, aligned):
    return jnp.dot(window_block, aligned, preferred_element_type=jnp.float32)


def shards(window, panels, row_map, panel_root, upper_blocks, diag_inverse, weights, pole_order):
    window_block = window[0]
    panel_slab = panels[0, 0]
    pole_roots = panel_root[0]
    band_rows = panel_slab.shape[0]
    group_rows = window_block.shape[0] // lax.axis_size("row")
    row_index = lax.axis_index("row")
    col_index = lax.axis_index("col")
    gathered_upper, gathered_inverse = (
        lax.all_gather(upper_blocks.astype(jnp.float32), "row", axis=2, tiled=True).astype(
            upper_blocks.dtype
        ),
        lax.all_gather(diag_inverse, "row", axis=2, tiled=True),
    )
    factors = gathered_upper[0].astype(jnp.float32)
    inverses = gathered_inverse[0]
    share_rows = inverses.shape[1] // lax.axis_size("row")
    slot_panels = lax.all_gather(panels, "col", axis=1, tiled=True)[0]
    pole_weight = jnp.sum(jnp.where(jnp.arange(weights.shape[0]) == pole_order[0], weights, 0.0))
    columns = []
    diagonals = []
    crossed = {}
    for current in range(NS):
        received = lax.dynamic_index_in_dim(slot_panels, pole_roots[current], 0, keepdims=False)
        aligned = jnp.take(received, row_map[current] - row_index * band_rows, axis=0)
        own_rows = lax.dynamic_slice_in_dim(aligned, col_index * group_rows, group_rows, 0).astype(
            jnp.float32
        )
        partials = [precise(columns[earlier].T, own_rows) for earlier in range(current)]
        window_sum = lax.psum_scatter(
            window_term(window_block, aligned), "row", scatter_dimension=0, tiled=True
        )
        y_window = window_sum
        for earlier in range(current):
            y_window = y_window + precise(columns[earlier], factors[pair_index(current, earlier)])
        congruence = precise(own_rows.T, y_window)
        stacked = lax.psum(jnp.stack(partials + [congruence]), ("row", "col"))
        summed_cross = stacked[:current]
        summed_own = stacked[current]
        y_blocks = []
        for earlier in range(current):
            block_sum = summed_cross[earlier]
            for other_node in range(current):
                block_sum = block_sum + precise(
                    inverse_block(diagonals, crossed, earlier, other_node),
                    factors[pair_index(current, other_node)],
                )
            y_blocks.append(block_sum)
        diagonal = inverses[current] + summed_own
        for earlier in range(current):
            diagonal = diagonal + precise(
                factors[pair_index(current, earlier)].T, y_blocks[earlier]
            )
            crossed[earlier, current] = -y_blocks[earlier]
        columns.append(-y_window)
        diagonals.append(diagonal)
    column_terms = jnp.stack(columns) * pole_weight
    diagonal_terms = (
        jnp.stack(
            [
                lax.dynamic_slice_in_dim(diagonal, row_index * share_rows, share_rows, 0)
                for diagonal in diagonals
            ]
        )
        * pole_weight
    )
    summed_columns, summed_diagonals = (
        lax.psum_scatter(column_terms, "pole", scatter_dimension=1, tiled=True),
        lax.psum_scatter(diagonal_terms, "pole", scatter_dimension=1, tiled=True),
    )
    return (summed_columns[:, None], summed_diagonals)


def solution(mesh):
    return jax.shard_map(
        shards,
        mesh=mesh,
        in_specs=(
            P("pole", "col", "row"),
            P("pole", "col", "row", None),
            P(None, "row"),
            P("pole", None),
            P("pole", None, "row", None),
            P("pole", None, "row", None),
            P(),
            P("pole"),
        ),
        out_specs=(P(None, "col", ("row", "pole"), None), P(None, ("row", "pole"), None)),
        check_vma=False,
    )
```

profile of v0, /device:TPU:0, one launch (start us, length us, event | category | flops | bytes accessed | tf_op | source)
XLA Modules:
  0.0 490.8 jit_solution(11846383781759528025)
XLA Ops:
  7.2 0.7 all-gather.2.cloned.1.call-update
  7.9 1.4 fusion.45
  15.1 0.9 slice_subtract_fusion.1
  16.0 29.3 %all-gather.2.cloned.1.call-done = bf16[1,2,2048,256]{3,2,0,1:T(8,128)(2,1)} async-done(((bf16[1,1,2048,256]{3,2,0,1:T(8,128)(2,1)}), bf16[1,2,2048,256]{3,2,0,1:T(8,128)(2,1)}) %all-gather.2.cloned.1.call-update) | async-done | bytes 2097168 | tf_op jit(solution)/shard_map/all_gather | solution.py:46
  45.4 2.2 dynamic-slice_bitcast_fusion.1
  47.6 9.0 %gather_fusion = bf16[2048,256]{1,0:T(8,128)(2,1)} fusion(bf16[2048,256]{1,0:T(8,128)(2,1)S(1)} %get-tuple-element.12, s32[2048]{0:T(1024)S(1)} %fusion.35), kind=kCustom, calls=%fused_computation.clone | custom fusion | bytes 2105344 | tf_op jit(solution)/shard_map/jit(_take)/gather | solution.py:53
  56.6 1.5 broadcast_select_fusion.2
  58.1 10.5 %fusion.6 = f32[4096,256]{0,1:T(8,128)} fusion(bf16[2048,256]{1,0:T(8,128)(2,1)S(1)} %broadcast_select_fusion.2, bf16[1,4096,2048]{2,1,0:T(8,128)(2,1)} %param.10), kind=kOutput, calls=%fused_computation.9 | convolution fusion | flops 4294967296 | bytes 22020096 | tf_op jit(solution)/shard_map/dot_general | solution.py:26
  68.7 7.5 %gather_fusion.1 = bf16[2048,256]{1,0:T(8,128)(2,1)S(1)} fusion(bf16[2048,256]{1,0:T(8,128)(2,1)S(1)} %get-tuple-element.10, s32[2048]{0:T(1024)S(1)} %fusion.36), kind=kCustom, calls=%fused_computation.1.clone | custom fusion | bytes 2105344 | tf_op jit(solution)/shard_map/jit(_take)/gather | solution.py:53
  76.2 0.4 broadcast_select_fusion.1
  76.7 10.6 %fusion.9 = f32[4096,256]{0,1:T(8,128)} fusion(bf16[2048,256]{1,0:T(8,128)(2,1)S(1)} %broadcast_select_fusion.1, bf16[1,4096,2048]{2,1,0:T(8,128)(2,1)} %param.10), kind=kOutput, calls=%fused_computation.10 | convolution fusion | flops 4294967296 | bytes 22020096 | tf_op jit(solution)/shard_map/dot_general | solution.py:26
  87.4 7.5 %gather_fusion.2 = bf16[2048,256]{1,0:T(8,128)(2,1)S(1)} fusion(bf16[2048,256]{1,0:T(8,128)(2,1)S(1)} %get-tuple-element.11, s32[2048]{0:T(1024)S(1)} %fusion.37), kind=kCustom, calls=%fused_computation.2.clone | custom fusion | bytes 2105344 | tf_op jit(solution)/shard_map/jit(_take)/gather | solution.py:53
  94.9 0.4 broadcast_select_fusion
  95.3 10.6 %fusion.12 = f32[4096,256]{0,1:T(8,128)} fusion(bf16[2048,256]{1,0:T(8,128)(2,1)S(1)} %broadcast_select_fusion, bf16[1,4096,2048]{2,1,0:T(8,128)(2,1)} %param.10), kind=kOutput, calls=%fused_computation.11 | convolution fusion | flops 4294967296 | bytes 22020096 | tf_op jit(solution)/shard_map/dot_general | solution.py:26
  106.0 0.8 copy-done.11
  106.8 20.3 %all_gather.10 = bf16[1,3,256,256]{3,2,1,0:T(8,128)(2,1)S(1)} all-gather(bf16[1,3,64,256]{3,2,1,0:T(8,128)(2,1)S(1)} %copy-done.11), channel_id=1, replica_groups=mesh['row'=4,'col'=2,'pole'=4] {'row'}, dimensions={2}, use_global_device_ids=true | all-gather | bytes 491520 | tf_op jit(solution)/shard_map/all_gather | solution.py:38
  127.2 24.6 %reduce-scatter.6.cloned.1.call-done = f32[1024,256]{0,1:T(8,128)} async-done(((f32[4096,256]{0,1:T(8,128)}), f32[1024,256]{0,1:T(8,128)}) %reduce-scatter.6.cloned.1.call-update) | async-done | bytes 1048592 | tf_op jit(solution)/shard_map/reduce_scatter | solution.py:58
  151.8 79.5 %reduce-scatter.8.cloned.1.call-done = f32[1024,256]{0,1:T(8,128)} async-done(((f32[4096,256]{0,1:T(8,128)}), f32[1024,256]{0,1:T(8,128)}) %reduce-scatter.8.cloned.1.call-update) | async-done | bytes 1048592 | tf_op jit(solution)/shard_map/reduce_scatter | solution.py:58
  231.3 2.2 convolution_add_fusion.2
  233.6 2.5 convolution_bitcast_fusion.6
  236.1 1.3 convolution_bitcast_fusion.4
  237.4 73.4 %reduce-scatter.10.cloned.1.call-done = f32[1024,256]{0,1:T(8,128)} async-done(((f32[4096,256]{0,1:T(8,128)}), f32[1024,256]{0,1:T(8,128)}) %reduce-scatter.10.cloned.1.call-update) | async-done | bytes 1048592 | tf_op jit(solution)/shard_map/reduce_scatter | solution.py:58
  310.8 2.1 convolution_add_fusion.1
  312.9 0.7 convolution_add_fusion
  313.7 0.8 convolution_bitcast_fusion.3
  314.4 0.6 convolution_bitcast_fusion.7
  315.1 0.8 pad_maximum_fusion.1
  315.9 0.6 convolution_bitcast_fusion.5
  316.6 0.9 pad_maximum_fusion
  317.5 1.5 convolution_bitcast_fusion.8
  319.7 0.6 fusion.44
  320.6 2.6 maximum_multiply_fusion
  323.3 31.1 %all_gather.11 = f32[1,3,256,256]{3,2,1,0:T(8,128)S(1)} all-gather(f32[1,3,64,256]{3,2,1,0:T(8,128)S(1)} %copy-done.10), channel_id=1, replica_groups=mesh['row'=4,'col'=2,'pole'=4] {'row'}, dimensions={2}, use_global_device_ids=true | all-gather | bytes 983040 | tf_op jit(solution)/shard_map/all_gather | solution.py:41
  354.4 67.3 %all-reduce.3.cloned.1.call-done = (f32[3,256,256]{2,1,0:T(8,128)}, f32[2,256,256]{2,1,0:T(8,128)}, f32[1,256,256]{2,1,0:T(8,128)}) async-done(((f32[3,256,256]{2,1,0:T(8,128)}, f32[2,256,256]{2,1,0:T(8,128)}, f32[1,256,256]{2,1,0:T(8,128)}), (f32[3,256,256]{2,1,0:T(8,128)}, f32[2,256,256]{2,1,0:T(8,128)}, f32[1,256,256]{2,1,0:T(8,128)})) %all-reduce.3.cloned.1.call-update) | async-done | bytes 1572880 | tf_op jit(solution)/shard_map/psum | solution.py:65
  421.8 0.9 fusion.34
  422.7 1.0 slice_bitcast_fusion.2
  423.6 1.3 convolution_add_fusion.6
  424.9 1.3 convolution_add_fusion.7
  426.3 0.3 convolution_add_fusion.5
  426.5 0.3 convolution_bitcast_fusion.1
  426.9 1.3 convolution_add_fusion.4
  428.2 0.3 fusion.15
  428.5 0.3 convolution_add_fusion.3
  428.8 0.3 convolution_bitcast_fusion
  429.2 1.3 maximum_multiply_fusion.1
  430.5 30.6 %reduce-scatter.12.cloned.1.call-done = f32[3,256,256]{1,2,0:T(8,128)} async-done(((f32[3,1024,256]{1,2,0:T(8,128)}), f32[3,256,256]{1,2,0:T(8,128)}) %reduce-scatter.12.cloned.1.call-update) | async-done | bytes 786448 | tf_op jit(solution)/shard_map/reduce_scatter | solution.py:96
  461.1 2.3 copy.18
  463.4 20.6 %reduce-scatter.14.cloned.1.call-done = f32[3,16,256]{2,1,0:T(8,128)} async-done(((f32[3,64,256]{2,1,0:T(8,128)}), f32[3,16,256]{2,1,0:T(8,128)}) %reduce-scatter.14.cloned.1.call-update) | async-done | bytes 49168 | tf_op jit(solution)/shard_map/reduce_scatter | solution.py:97
  (48 shorter events, 0.8 us)
Async XLA Ops:
  7.2 38.2 %all-gather.2.cloned.1.call-start = ((), (), s32[]{:S(2)}) async-start(), calls=%async_computation.5 | async-start | bytes 3145728 | tf_op jit(solution)/shard_map/all_gather | solution.py:46
  7.9 143.9 %reduce-scatter.6.cloned.1.call-start = ((), (), s32[]{:S(2)}) async-start(), calls=%async_computation.6 | async-start | bytes 5242880 | tf_op jit(solution)/shard_map/reduce_scatter | solution.py:58
  58.1 10.5 %copy-start.5 = (bf16[2048,256]{1,0:T(8,128)(2,1)}, bf16[2048,256]{1,0:T(8,128)(2,1)S(1)}, u32[]{:S(2)}) copy-start(bf16[2048,256]{1,0:T(8,128)(2,1)S(1)} %broadcast_select_fusion.2) | copy-start | bytes 3145732
  68.6 162.7 %reduce-scatter.8.cloned.1.call-start = ((), (), s32[]{:S(2)}) async-start(), calls=%async_computation.7 | async-start | bytes 5242880 | tf_op jit(solution)/shard_map/reduce_scatter | solution.py:58
  76.7 10.6 %copy-start.3 = (bf16[2048,256]{1,0:T(8,128)(2,1)}, bf16[2048,256]{1,0:T(8,128)(2,1)S(1)}, u32[]{:S(2)}) copy-start(bf16[2048,256]{1,0:T(8,128)(2,1)S(1)} %broadcast_select_fusion.1) | copy-start | bytes 3145732
  87.3 223.5 %reduce-scatter.10.cloned.1.call-start = ((), (), s32[]{:S(2)}) async-start(), calls=%async_computation.8 | async-start | bytes 5242880 | tf_op jit(solution)/shard_map/reduce_scatter | solution.py:58
  95.3 140.8 %copy-start.1 = (bf16[2048,256]{1,0:T(8,128)(2,1)}, bf16[2048,256]{1,0:T(8,128)(2,1)S(1)}, u32[]{:S(2)}) copy-start(bf16[2048,256]{1,0:T(8,128)(2,1)S(1)} %broadcast_select_fusion) | copy-start | bytes 3145732
  105.9 0.9 copy-start.11
  105.9 315.8 %all-reduce.3.cloned.1.call-start = ((), (), s32[]{:S(2)}) async-start(), calls=%async_computation.11 | async-start | bytes 3145728 | tf_op jit(solution)/shard_map/psum | solution.py:65
  151.8 159.0 %copy-start = (f32[1024,256]{0,1:T(8,128)S(1)}, f32[1024,256]{0,1:T(8,128)}, u32[]{:S(2)}) copy-start(f32[1024,256]{0,1:T(8,128)} %reduce-scatter.6.cloned.1.call-done) | copy-start | bytes 3145732
  310.8 2.8 copy-start.2
  310.8 3.6 copy-start.4
  312.9 2.2 copy-start.8
  312.9 3.7 copy-start.7
  313.6 3.9 copy-start.6
  315.1 4.6 copy-start.12
  319.0 142.1 %reduce-scatter.12.cloned.1.call-start = ((), (), s32[]{:S(2)}) async-start(), calls=%async_computation.9 | async-start | bytes 3932160 | tf_op jit(solution)/shard_map/reduce_scatter | solution.py:96
  320.6 2.6 copy-start.10
  323.2 160.7 %reduce-scatter.14.cloned.1.call-start = ((), (), s32[]{:S(2)}) async-start(), calls=%async_computation.10 | async-start | bytes 245760 | tf_op jit(solution)/shard_map/reduce_scatter | solution.py:97
  421.8 6.5 %copy-start.9 = (f32[2,256,256]{2,1,0:T(8,128)S(1)}, f32[2,256,256]{2,1,0:T(8,128)}, u32[]{:S(2)}) copy-start(f32[2,256,256]{2,1,0:T(8,128)} %get-tuple-element.8) | copy-start | bytes 1572868
Sparse Core Ops, SparseCore 0:
  9.5 35.8 all-gather.1
  68.8 82.9 reduce-scatter.5
  154.1 77.2 reduce-scatter.7
  233.5 77.2 reduce-scatter.9
  319.2 102.5 all-reduce.2
  424.1 36.9 reduce-scatter.11
  464.1 19.7 reduce-scatter.13
where the time goes:
time: 491 us
  waiting for transfers between devices  326 us (66%)
  blocking collectives  51.5 us (10%)
  matrix products  49.5 us (10%)
  local copies, waits for them, and re-layouts  31.8 us (6%)
  between operations  20.9 us (4%)
  other arithmetic  10.7 us (2%)
    reduce_scatter x3, waiting for transfers between devices, shards(): lax.psum_scatter(window_term(window_block, aligned), 'row', scatter_dimen...  178 us
    psum x1, waiting for transfers between devices, shards(): stacked = lax.psum(jnp.stack(partials + [congruence]), ('row', 'col'))  67.3 us
    dot_general x3, matrix products, window_term(): return jnp.dot(window_block, aligned, preferred_element_type=jnp.float32)  31.7 us
    all_gather x1, blocking collectives, shards(): lax.all_gather(diag_inverse, 'row', axis=2, tiled=True)  31.1 us
    reduce_scatter x1, waiting for transfers between devices, shards(): lax.psum_scatter(column_terms, 'pole', scatter_dimension=1, tiled=True)  30.6 us
    all_gather x1, waiting for transfers between devices, shards(): slot_panels = lax.all_gather(panels, 'col', axis=1, tiled=True)[0]  29.3 us
    gather x3, local copies, waits for them, and re-layouts, shards(): jnp.take(received, row_map[current] - row_index * band_rows, axis=0)  24 us
    reduce_scatter x1, waiting for transfers between devices, shards(): lax.psum_scatter(diagonal_terms, 'pole', scatter_dimension=1, tiled=True)  20.6 us
  transfers between devices with their start and end apart: 7, of which 7 were waited for; matrix products, arithmetic and copies ran while one was open for 12% of the time, Pallas kernels for 0%

commit v1 on v0

--- a/solution.py
+++ b/solution.py
@@ -62,7 +62,7 @@
         for earlier in range(current):
             y_window = y_window + precise(columns[earlier], factors[pair_index(current, earlier)])
         congruence = precise(own_rows.T, y_window)
-        stacked = lax.psum(jnp.stack(partials + [congruence]), ("row", "col"))
+        stacked = lax.psum(lax.psum(jnp.stack(partials + [congruence]), "row"), "col")
         summed_cross = stacked[:current]
         summed_own = stacked[current]
         y_blocks = []

time: 491 us -> 512 us (1.043)
  waiting for transfers between devices: 326 us -> 360 us
  blocking collectives: 51.5 us -> 38.2 us
    psum x1 -> x2, waiting for transfers between devices: 67.3 us -> 100 us  [the longest x1 69.7 us: shards(): lax.psum(jnp.stack(partials + [congruence]), 'row')]
    all_gather x1, blocking collectives: 31.1 us -> 17.9 us  [shards(): lax.all_gather(diag_inverse, 'row', axis=2, tiled=True)]
  transfers between devices with their start and end apart: 7 -> 8, of which waited for: 7 -> 8; matrix products, arithmetic and copies ran while one was open for 12% -> 12% of each run, Pallas kernels for 0% -> 0%
where the time goes in v1:
time: 512 us
  waiting for transfers between devices  360 us (70%)
  matrix products  49.6 us (10%)
  blocking collectives  38.2 us (7%)
  local copies, waits for them, and re-layouts  31.8 us (6%)
  between operations  20.9 us (4%)
  other arithmetic  10.9 us (2%)
    reduce_scatter x3, waiting for transfers between devices, shards(): lax.psum_scatter(window_term(window_block, aligned), 'row', scatter_dimen...  178 us
    psum x1, waiting for transfers between devices, shards(): lax.psum(jnp.stack(partials + [congruence]), 'row')  69.7 us
    dot_general x3, matrix products, window_term(): return jnp.dot(window_block, aligned, preferred_element_type=jnp.float32)  31.7 us
    reduce_scatter x1, waiting for transfers between devices, shards(): lax.psum_scatter(column_terms, 'pole', scatter_dimension=1, tiled=True)  31.5 us
    psum x1, waiting for transfers between devices, shards(): lax.psum(lax.psum(jnp.stack(partials + [congruence]), 'row'), 'col')  30.6 us
    all_gather x1, waiting for transfers between devices, shards(): slot_panels = lax.all_gather(panels, 'col', axis=1, tiled=True)[0]  29.3 us
    gather x3, local copies, waits for them, and re-layouts, shards(): jnp.take(received, row_map[current] - row_index * band_rows, axis=0)  24 us
    reduce_scatter x1, waiting for transfers between devices, shards(): lax.psum_scatter(diagonal_terms, 'pole', scatter_dimension=1, tiled=True)  20.5 us
  transfers between devices with their start and end apart: 8, of which 8 were waited for; matrix products, arithmetic and copies ran while one was open for 12% of the time, Pallas kernels for 0%

profile of v1, /device:TPU:0, one launch (start us, length us, event | category | flops | bytes accessed | tf_op | source)
XLA Modules:
  0.0 511.7 jit_solution(18328406704350297020)
XLA Ops:
  7.2 0.7 all-gather.2.cloned.1.call-update
  7.9 1.4 fusion.45
  15.1 0.9 slice_subtract_fusion.1
  16.0 29.3 %all-gather.2.cloned.1.call-done = bf16[1,2,2048,256]{3,2,0,1:T(8,128)(2,1)} async-done(((bf16[1,1,2048,256]{3,2,0,1:T(8,128)(2,1)}), bf16[1,2,2048,256]{3,2,0,1:T(8,128)(2,1)}) %all-gather.2.cloned.1.call-update) | async-done | bytes 2097168 | tf_op jit(solution)/shard_map/all_gather | solution.py:46
  45.4 2.3 dynamic-slice_bitcast_fusion.1
  47.6 9.0 %gather_fusion = bf16[2048,256]{1,0:T(8,128)(2,1)} fusion(bf16[2048,256]{1,0:T(8,128)(2,1)S(1)} %get-tuple-element.15, s32[2048]{0:T(1024)S(1)} %fusion.35), kind=kCustom, calls=%fused_computation.clone | custom fusion | bytes 2105344 | tf_op jit(solution)/shard_map/jit(_take)/gather | solution.py:53
  56.6 1.5 broadcast_select_fusion.2
  58.1 10.5 %fusion.6 = f32[4096,256]{0,1:T(8,128)} fusion(bf16[2048,256]{1,0:T(8,128)(2,1)S(1)} %broadcast_select_fusion.2, bf16[1,4096,2048]{2,1,0:T(8,128)(2,1)} %param.10), kind=kOutput, calls=%fused_computation.9 | convolution fusion | flops 4294967296 | bytes 22020096 | tf_op jit(solution)/shard_map/dot_general | solution.py:26
  68.7 7.5 %gather_fusion.1 = bf16[2048,256]{1,0:T(8,128)(2,1)S(1)} fusion(bf16[2048,256]{1,0:T(8,128)(2,1)S(1)} %get-tuple-element.13, s32[2048]{0:T(1024)S(1)} %fusion.36), kind=kCustom, calls=%fused_computation.1.clone | custom fusion | bytes 2105344 | tf_op jit(solution)/shard_map/jit(_take)/gather | solution.py:53
  76.3 0.4 broadcast_select_fusion.1
  76.7 10.6 %fusion.9 = f32[4096,256]{0,1:T(8,128)} fusion(bf16[2048,256]{1,0:T(8,128)(2,1)S(1)} %broadcast_select_fusion.1, bf16[1,4096,2048]{2,1,0:T(8,128)(2,1)} %param.10), kind=kOutput, calls=%fused_computation.10 | convolution fusion | flops 4294967296 | bytes 22020096 | tf_op jit(solution)/shard_map/dot_general | solution.py:26
  87.4 7.5 %gather_fusion.2 = bf16[2048,256]{1,0:T(8,128)(2,1)S(1)} fusion(bf16[2048,256]{1,0:T(8,128)(2,1)S(1)} %get-tuple-element.14, s32[2048]{0:T(1024)S(1)} %fusion.37), kind=kCustom, calls=%fused_computation.2.clone | custom fusion | bytes 2105344 | tf_op jit(solution)/shard_map/jit(_take)/gather | solution.py:53
  94.9 0.4 broadcast_select_fusion
  95.4 10.6 %fusion.12 = f32[4096,256]{0,1:T(8,128)} fusion(bf16[2048,256]{1,0:T(8,128)(2,1)S(1)} %broadcast_select_fusion, bf16[1,4096,2048]{2,1,0:T(8,128)(2,1)} %param.10), kind=kOutput, calls=%fused_computation.11 | convolution fusion | flops 4294967296 | bytes 22020096 | tf_op jit(solution)/shard_map/dot_general | solution.py:26
  106.0 0.8 copy-done.11
  106.8 20.3 %all_gather.10 = bf16[1,3,256,256]{3,2,1,0:T(8,128)(2,1)S(1)} all-gather(bf16[1,3,64,256]{3,2,1,0:T(8,128)(2,1)S(1)} %copy-done.11), channel_id=1, replica_groups=mesh['row'=4,'col'=2,'pole'=4] {'row'}, dimensions={2}, use_global_device_ids=true | all-gather | bytes 491520 | tf_op jit(solution)/shard_map/all_gather | solution.py:38
  127.2 24.6 %reduce-scatter.6.cloned.1.call-done = f32[1024,256]{0,1:T(8,128)} async-done(((f32[4096,256]{0,1:T(8,128)}), f32[1024,256]{0,1:T(8,128)}) %reduce-scatter.6.cloned.1.call-update) | async-done | bytes 1048592 | tf_op jit(solution)/shard_map/reduce_scatter | solution.py:58
  151.8 79.6 %reduce-scatter.8.cloned.1.call-done = f32[1024,256]{0,1:T(8,128)} async-done(((f32[4096,256]{0,1:T(8,128)}), f32[1024,256]{0,1:T(8,128)}) %reduce-scatter.8.cloned.1.call-update) | async-done | bytes 1048592 | tf_op jit(solution)/shard_map/reduce_scatter | solution.py:58
  231.3 2.2 convolution_add_fusion.2
  233.6 2.5 convolution_bitcast_fusion.6
  236.1 1.3 convolution_bitcast_fusion.4
  237.5 73.4 %reduce-scatter.10.cloned.1.call-done = f32[1024,256]{0,1:T(8,128)} async-done(((f32[4096,256]{0,1:T(8,128)}), f32[1024,256]{0,1:T(8,128)}) %reduce-scatter.10.cloned.1.call-update) | async-done | bytes 1048592 | tf_op jit(solution)/shard_map/reduce_scatter | solution.py:58
  310.8 2.1 convolution_add_fusion.1
  312.9 0.7 convolution_add_fusion
  313.7 0.8 convolution_bitcast_fusion.3
  314.5 0.6 convolution_bitcast_fusion.7
  315.1 0.8 pad_maximum_fusion.1
  316.0 0.6 convolution_bitcast_fusion.5
  316.6 0.9 pad_maximum_fusion
  317.6 1.5 convolution_bitcast_fusion.8
  319.1 69.7 %all-reduce.5.cloned.1.call-done = (f32[3,256,256]{2,1,0:T(8,128)}, f32[2,256,256]{2,1,0:T(8,128)}, f32[1,256,256]{2,1,0:T(8,128)}) async-done(((f32[3,256,256]{2,1,0:T(8,128)}, f32[2,256,256]{2,1,0:T(8,128)}, f32[1,256,256]{2,1,0:T(8,128)}), (f32[3,256,256]{2,1,0:T(8,128)}, f32[2,256,256]{2,1,0:T(8,128)}, f32[1,256,256]{2,1,0:T(8,128)})) %all-reduce.5.cloned.1.call-update) | async-done | bytes 1572880 | tf_op jit(solution)/shard_map/psum | solution.py:65
  389.5 0.6 fusion.44
  390.4 2.6 maximum_multiply_fusion
  393.2 17.9 %all_gather.11 = f32[1,3,256,256]{3,2,1,0:T(8,128)S(1)} all-gather(f32[1,3,64,256]{3,2,1,0:T(8,128)S(1)} %copy-done.10), channel_id=1, replica_groups=mesh['row'=4,'col'=2,'pole'=4] {'row'}, dimensions={2}, use_global_device_ids=true | all-gather | bytes 983040 | tf_op jit(solution)/shard_map/all_gather | solution.py:41
  411.1 30.6 %all-reduce.7.cloned.1.call-done = (f32[3,256,256]{2,1,0:T(8,128)}, f32[2,256,256]{2,1,0:T(8,128)}, f32[1,256,256]{2,1,0:T(8,128)}) async-done(((f32[3,256,256]{2,1,0:T(8,128)}, f32[2,256,256]{2,1,0:T(8,128)}, f32[1,256,256]{2,1,0:T(8,128)}), (f32[3,256,256]{2,1,0:T(8,128)}, f32[2,256,256]{2,1,0:T(8,128)}, f32[1,256,256]{2,1,0:T(8,128)})) %all-reduce.7.cloned.1.call-update) | async-done | bytes 1572880 | tf_op jit(solution)/shard_map/psum | solution.py:65
  441.7 0.9 fusion.34
  442.6 1.0 slice_bitcast_fusion.2
  443.6 1.3 convolution_add_fusion.6
  444.9 1.3 convolution_add_fusion.7
  446.5 0.3 convolution_bitcast_fusion.1
  446.8 1.3 convolution_add_fusion.4
  448.2 0.3 fusion.15
  448.5 0.3 convolution_add_fusion.3
  448.8 0.3 convolution_bitcast_fusion
  449.2 1.3 maximum_multiply_fusion.1
  450.5 31.5 %reduce-scatter.12.cloned.1.call-done = f32[3,256,256]{1,2,0:T(8,128)} async-done(((f32[3,1024,256]{1,2,0:T(8,128)}), f32[3,256,256]{1,2,0:T(8,128)}) %reduce-scatter.12.cloned.1.call-update) | async-done | bytes 786448 | tf_op jit(solution)/shard_map/reduce_scatter | solution.py:96
  482.0 2.3 copy.18
  484.3 20.5 %reduce-scatter.14.cloned.1.call-done = f32[3,16,256]{2,1,0:T(8,128)} async-done(((f32[3,64,256]{2,1,0:T(8,128)}), f32[3,16,256]{2,1,0:T(8,128)}) %reduce-scatter.14.cloned.1.call-update) | async-done | bytes 49168 | tf_op jit(solution)/shard_map/reduce_scatter | solution.py:97
  (51 shorter events, 1.2 us)
Async XLA Ops:
  7.2 38.2 %all-gather.2.cloned.1.call-start = ((), (), s32[]{:S(2)}) async-start(), calls=%async_computation.5 | async-start | bytes 3145728 | tf_op jit(solution)/shard_map/all_gather | solution.py:46
  7.9 143.9 %reduce-scatter.6.cloned.1.call-start = ((), (), s32[]{:S(2)}) async-start(), calls=%async_computation.6 | async-start | bytes 5242880 | tf_op jit(solution)/shard_map/reduce_scatter | solution.py:58
  58.1 10.5 %copy-start.5 = (bf16[2048,256]{1,0:T(8,128)(2,1)}, bf16[2048,256]{1,0:T(8,128)(2,1)S(1)}, u32[]{:S(2)}) copy-start(bf16[2048,256]{1,0:T(8,128)(2,1)S(1)} %broadcast_select_fusion.2) | copy-start | bytes 3145732
  68.7 162.7 %reduce-scatter.8.cloned.1.call-start = ((), (), s32[]{:S(2)}) async-start(), calls=%async_computation.7 | async-start | bytes 5242880 | tf_op jit(solution)/shard_map/reduce_scatter | solution.py:58
  76.7 10.6 %copy-start.3 = (bf16[2048,256]{1,0:T(8,128)(2,1)}, bf16[2048,256]{1,0:T(8,128)(2,1)S(1)}, u32[]{:S(2)}) copy-start(bf16[2048,256]{1,0:T(8,128)(2,1)S(1)} %broadcast_select_fusion.1) | copy-start | bytes 3145732
  87.3 223.5 %reduce-scatter.10.cloned.1.call-start = ((), (), s32[]{:S(2)}) async-start(), calls=%async_computation.8 | async-start | bytes 5242880 | tf_op jit(solution)/shard_map/reduce_scatter | solution.py:58
  95.4 140.8 %copy-start.1 = (bf16[2048,256]{1,0:T(8,128)(2,1)}, bf16[2048,256]{1,0:T(8,128)(2,1)S(1)}, u32[]{:S(2)}) copy-start(bf16[2048,256]{1,0:T(8,128)(2,1)S(1)} %broadcast_select_fusion) | copy-start | bytes 3145732
  106.0 0.9 copy-start.11
  106.0 282.8 %all-reduce.5.cloned.1.call-start = ((), (), s32[]{:S(2)}) async-start(), calls=%async_computation.11 | async-start | bytes 3145728 | tf_op jit(solution)/shard_map/psum | solution.py:65
  151.8 159.1 %copy-start = (f32[1024,256]{0,1:T(8,128)S(1)}, f32[1024,256]{0,1:T(8,128)}, u32[]{:S(2)}) copy-start(f32[1024,256]{0,1:T(8,128)} %reduce-scatter.6.cloned.1.call-done) | copy-start | bytes 3145732
  310.8 2.8 copy-start.2
  310.8 3.6 copy-start.4
  312.9 2.2 copy-start.8
  312.9 3.7 copy-start.7
  313.7 3.9 copy-start.6
  316.0 73.5 %copy-start.12 = (f32[4]{0:T(128)S(1)}, f32[4]{0:T(128)}, u32[]{:S(2)}) copy-start(f32[4]{0:T(128)} %param.16) | copy-start | bytes 52
  319.1 122.7 %all-reduce.7.cloned.1.call-start = ((), (), s32[]{:S(2)}) async-start(), calls=%async_computation.12 | async-start | bytes 3145728 | tf_op jit(solution)/shard_map/psum | solution.py:65
  388.8 93.2 %reduce-scatter.12.cloned.1.call-start = ((), (), s32[]{:S(2)}) async-start(), calls=%async_computation.9 | async-start | bytes 3932160 | tf_op jit(solution)/shard_map/reduce_scatter | solution.py:96
  390.4 2.7 copy-start.10
  393.1 111.8 %reduce-scatter.14.cloned.1.call-start = ((), (), s32[]{:S(2)}) async-start(), calls=%async_computation.10 | async-start | bytes 245760 | tf_op jit(solution)/shard_map/reduce_scatter | solution.py:97
  441.7 6.5 %copy-start.9 = (f32[2,256,256]{2,1,0:T(8,128)S(1)}, f32[2,256,256]{2,1,0:T(8,128)}, u32[]{:S(2)}) copy-start(f32[2,256,256]{2,1,0:T(8,128)} %get-tuple-element.11) | copy-start | bytes 1572868
Sparse Core Ops, SparseCore 0:
  9.5 35.8 all-gather.1
  68.8 82.9 reduce-scatter.5
  154.1 77.2 reduce-scatter.7
  233.5 77.2 reduce-scatter.9
  319.2 69.5 all-reduce.4
  391.0 50.6 all-reduce.6
  444.3 37.7 reduce-scatter.11
  485.1 19.7 reduce-scatter.13
